TPU v7x, 32 devices: a whole 2x2x4 slice. The times are simulated.
32 devices in a mesh: replica: 8 (over y, x, core), tensor: 4 (over z).
Axes of the slice: x: 2, y: 2, z: 4, core: 2. Of those that a mesh axis runs over, the one named last changes fastest.
Arguments:
- weights: bfloat16 [8, 8192, 2048], P('replica', 'tensor'), may hold values from -6 to 6
- hidden: bfloat16 [8, 512, 8192], P('replica', None, 'tensor'), may hold values from -6 to 6
- out_grad: bfloat16 [8, 512, 2048], P('replica', None, 'tensor'), may hold values from -0.375 to 0.375
- factor_start: bfloat16 [2, 64, 8192], P(None, None, 'tensor'), may hold values from -6 to 6
- matching: int32 [2], replicated, may hold values from 1 to 7, as said below
Outputs:
- new_weights: bfloat16 [8, 8192, 2048], P('replica', 'tensor')
Inputs may be any that keep to these rules, and one draw needn't show every extreme that they name: In step t replica i is matched with replica i XOR matching[t]; in one of the steps matching equals 7.
All inputs are finite; a program needn't handle non-finite values.
Results may differ from a plain program's by a relative error of at most 0.014.
Values may be sent and summed in bfloat16 or wider, within the bound.
No kernel may reach another device: no remote copies, remote signals or barrier semaphores. Data moves between devices by JAX's collectives and lax.ppermute only.
A program may use at most 128 MiB of HBM per device.

v0:
```python
import jax
import jax.numpy as jnp
from jax import lax
from jax.sharding import PartitionSpec as P

STEPS = 2
TOK = 256
learn_rate = 0.1
momentum_decay = 0.9


def from_partner(value, axis, bit):
    mask = 2**bit
    pairs = [(source, source ^ mask) for source in range(lax.axis_size(axis))]
    return lax.ppermute(value, axis, pairs)


def swap_left_side(payload, pairing):
    for bit_number in range(lax.axis_size("replica").bit_length() - 1):
        arrived = from_partner(payload.astype(jnp.bfloat16), "replica", bit_number).astype(
            payload.dtype
        )
        chosen = pairing // 2**bit_number % 2
        payload = jnp.where(chosen == 1, arrived, payload)
    return payload


def swap_right_side(payload, pairing):
    for bit_number in range(lax.axis_size("replica").bit_length() - 1):
        arrived = from_partner(payload.astype(jnp.bfloat16), "replica", bit_number).astype(
            payload.dtype
        )
        chosen = pairing // 2**bit_number % 2
        payload = jnp.where(chosen == 1, arrived, payload)
    return payload


def orthonormal(gram_matrix, difference):
    lower_factor = jnp.linalg.cholesky(gram_matrix)
    return lax.linalg.triangular_solve(lower_factor, difference, left_side=True, lower=True)


def per_device(weights, hidden, out_grad, factor_start, matching):
    current = weights[0]
    hidden_all = hidden[0]
    grads_all = out_grad[0]
    momentum = None
    for step_index in range(STEPS):
        hidden_step = hidden_all[step_index * TOK : (step_index + 1) * TOK]
        grads_step = grads_all[step_index * TOK : (step_index + 1) * TOK]
        gradient = lax.dot_general(
            hidden_step,
            lax.all_gather(grads_step, "tensor", axis=1, tiled=True),
            (((0,), (0,)), ((), ())),
            preferred_element_type=jnp.float32,
        )
        if momentum is None:
            momentum = gradient
        else:
            momentum = momentum_decay * momentum + gradient
        updated = (current.astype(jnp.float32) - learn_rate * momentum).astype(jnp.bfloat16)
        start_factor = factor_start[step_index]
        pairing = matching[step_index]
        local_left = jnp.dot(start_factor, updated, preferred_element_type=jnp.float32)
        left_total = lax.psum(local_left.astype(jnp.bfloat16), "tensor").astype(jnp.float32)
        left_diff = left_total - swap_left_side(left_total, pairing)
        gram_matrix = jnp.dot(left_diff, left_diff.T, precision=lax.Precision.HIGHEST)
        ortho_bf = orthonormal(gram_matrix, left_diff).astype(jnp.bfloat16)
        right_prod = lax.dot_general(
            ortho_bf, updated, (((1,), (1,)), ((), ())), preferred_element_type=jnp.float32
        )
        right_diff = (right_prod - swap_right_side(right_prod, pairing)).astype(jnp.bfloat16)
        change = lax.dot_general(
            right_diff, ortho_bf, (((0,), (0,)), ((), ())), preferred_element_type=jnp.float32
        )
        current = (updated.astype(jnp.float32) - 0.5 * change).astype(jnp.bfloat16)
    return current[None]


def solution(mesh):
    return jax.shard_map(
        per_device,
        mesh=mesh,
        in_specs=(
            P("replica", "tensor", None),
            P("replica", None, "tensor"),
            P("replica", None, "tensor"),
            P(None, None, "tensor"),
            P(),
        ),
        out_specs=P("replica", "tensor", None),
        check_vma=False,
    )
```

profile of v0, /device:TPU:0, one launch (start us, length us, event | category | flops | bytes accessed | tf_op | source)
XLA Modules:
  0.0 294.4 jit_solution(8720896719160545904)
XLA Ops:
  6.5 1.9 fusion.37
  8.5 31.2 %all-gather.5.cloned.1.call-done = bf16[1,256,2048]{2,1,0:T(8,128)(2,1)} async-done(((bf16[1,256,512]{2,1,0:T(8,128)(2,1)}), bf16[1,256,2048]{2,1,0:T(8,128)(2,1)}) %all-gather.5.cloned.1.call-update) | async-done | bytes 1048592 | tf_op jit(solution)/shard_map/all_gather | solution.py:53
  39.6 12.2 %fusion = (bf16[2048,2048]{1,0:T(8,128)(2,1)S(1)}, f32[2048,2048]{1,0:T(8,128)}) fusion(bf16[1,2048,2048]{2,1,0:T(8,128)(2,1)} %param.8, bf16[1,256,2048]{2,1,0:T(8,128)(2,1)} %all-gather.5.cloned.1.call-done, bf16[1,512,2048]{2,1,0:T(8,128)(2,1)} %param.9), kind=kOutput, calls=%fused_computation.1 | convolution fusion | flops 2164260864 | bytes 35651584 | tf_op jit(solution)/shard_map/dot_general | solution.py:51
  51.8 3.4 %copy-done = bf16[2048,2048]{1,0:T(8,128)(2,1)} copy-done((bf16[2048,2048]{1,0:T(8,128)(2,1)}, bf16[2048,2048]{1,0:T(8,128)(2,1)S(1)}, u32[]{:S(2)}) %copy-start) | copy-done | bytes 8388632
  55.2 2.3 fusion.2
  57.6 34.9 %all-reduce.3.cloned.1.call-done = bf16[64,2048]{1,0:T(8,128)(2,1)} async-done(((bf16[64,2048]{1,0:T(8,128)(2,1)}), bf16[64,2048]{1,0:T(8,128)(2,1)}) %all-reduce.3.cloned.1.call-update) | async-done | bytes 262160 | tf_op jit(solution)/shard_map/psum | solution.py:65
  98.5 6.5 %collective-permute-done.1 = bf16[64,2048]{1,0:T(8,128)(2,1)S(1)} collective-permute-done((bf16[64,2048]{1,0:T(8,128)(2,1)S(1)}, bf16[64,2048]{1,0:T(8,128)(2,1)S(1)}, u32[]{:S(2)}, u32[]{:S(2)}) %collective-permute-start.1) | collective-permute-done | bytes 262176 | tf_op jit(solution)/shard_map/ppermute | solution.py:15
  107.6 6.4 %collective-permute-done.2 = bf16[64,2048]{1,0:T(8,128)(2,1)S(1)} collective-permute-done((bf16[64,2048]{1,0:T(8,128)(2,1)S(1)}, bf16[64,2048]{1,0:T(8,128)(2,1)S(1)}, u32[]{:S(2)}, u32[]{:S(2)}) %collective-permute-start.2) | collective-permute-done | bytes 262176 | tf_op jit(solution)/shard_map/ppermute | solution.py:15
  114.0 1.8 fusion.29
  115.9 5.8 %cholesky.44 = f32[64,64]{1,0:T(8,128)S(1)} custom-call(f32[64,64]{1,0:T(8,128)S(1)} %fusion.36), custom_call_target="Cholesky" | custom-call | tf_op jit(solution)/shard_map/jit(cholesky)/cholesky | solution.py:39
  123.3 4.9 %custom-call.6 = f32[1,64,64]{1,2,0:T(8,128)S(1)} custom-call(f32[1,64,64]{2,1,0:T(8,128)S(1)} %fusion.31), custom_call_target="InvertDiagBlocksLowerTriangular" | custom-call | tf_op jit(solution)/shard_map/triangular_solve/custom-call.0 | solution.py:40
  128.2 1.7 convolution_convert_fusion.3
  129.8 6.0 %fusion.39 = (bf16[64,2048]{1,0:T(8,128)(2,1)S(1)}, f32[64,2048]{1,0:T(8,128)S(1)}) fusion(bf16[64,2048]{1,0:T(8,128)(2,1)S(1)} %convolution_convert_fusion.3, bf16[2048,2048]{1,0:T(8,128)(2,1)} %copy-done), kind=kOutput, calls=%fused_computation.69 | convolution fusion | flops 537001984 | bytes 9437184 | tf_op jit(solution)/shard_map/dot_general | solution.py:69
  139.3 6.6 %collective-permute-done.4 = bf16[64,2048]{1,0:T(8,128)(2,1)S(1)} collective-permute-done((bf16[64,2048]{1,0:T(8,128)(2,1)S(1)}, bf16[64,2048]{1,0:T(8,128)(2,1)S(1)}, u32[]{:S(2)}, u32[]{:S(2)}) %collective-permute-start.4) | collective-permute-done | bytes 262176 | tf_op jit(solution)/shard_map/ppermute | solution.py:15
  146.0 1.5 collective-permute-start.5
  147.6 6.0 %collective-permute-done.5 = bf16[64,2048]{1,0:T(8,128)(2,1)S(1)} collective-permute-done((bf16[64,2048]{1,0:T(8,128)(2,1)S(1)}, bf16[64,2048]{1,0:T(8,128)(2,1)S(1)}, u32[]{:S(2)}, u32[]{:S(2)}) %collective-permute-start.5) | collective-permute-done | bytes 262176 | tf_op jit(solution)/shard_map/ppermute | solution.py:15
  153.6 6.9 %subtract_convert_fusion.2 = bf16[2048,2048]{1,0:T(8,128)(2,1)} fusion(bf16[2048,2048]{1,0:T(8,128)(2,1)} %copy-done, bf16[64,2048]{1,0:T(8,128)(2,1)S(1)} %convolution_convert_fusion.3, f32[64,2048]{1,0:T(8,128)S(1)} %get-tuple-element.14, bf16[64,2048]{1,0:T(8,128)(2,1)S(1)} %collective-permute-done.5, bf16[64,2048]{1,0:T(8,128)(2,1)S(1)} %collective-permute-done.3, ...), kind=kOutput, calls=%fused_computation.4 | convolution fusion | flops 554696704 | bytes 18350084 | tf_op jit(solution)/shard_map/dot_general | solution.py:73
  160.5 5.7 %all-gather.7.cloned.1.call-done = bf16[1,256,2048]{2,1,0:T(8,128)(2,1)} async-done(((bf16[1,256,512]{2,1,0:T(8,128)(2,1)}), bf16[1,256,2048]{2,1,0:T(8,128)(2,1)}) %all-gather.7.cloned.1.call-update) | async-done | bytes 1048592 | tf_op jit(solution)/shard_map/all_gather | solution.py:53
  166.2 14.0 %subtract_convert_fusion.1 = bf16[2048,2048]{1,0:T(8,128)(2,1)} fusion(f32[2048,2048]{1,0:T(8,128)} %get-tuple-element.12, bf16[2048,2048]{1,0:T(8,128)(2,1)} %subtract_convert_fusion.2, bf16[1,256,2048]{2,1,0:T(8,128)(2,1)} %all-gather.7.cloned.1.call-done, bf16[1,512,2048]{2,1,0:T(8,128)(2,1)S(1)} %copy-done.1), kind=kOutput, calls=%fused_computation.3 | convolution fusion | flops 2172649472 | bytes 35651584 | tf_op jit(solution)/shard_map/dot_general | solution.py:51
  180.2 5.6 %fusion.3 = bf16[64,2048]{1,0:T(8,128)(2,1)} fusion(bf16[2048,2048]{1,0:T(8,128)(2,1)} %subtract_convert_fusion.1, bf16[2,64,2048]{2,1,0:T(8,128)(2,1)S(1)} %copy-done.3), kind=kOutput, calls=%fused_computation.11 | convolution fusion | flops 537001984 | bytes 8912896 | tf_op jit(solution)/shard_map/dot_general | solution.py:64
  185.8 35.1 %all-reduce.5.cloned.1.call-done = bf16[64,2048]{1,0:T(8,128)(2,1)} async-done(((bf16[64,2048]{1,0:T(8,128)(2,1)}), bf16[64,2048]{1,0:T(8,128)(2,1)}) %all-reduce.5.cloned.1.call-update) | async-done | bytes 262160 | tf_op jit(solution)/shard_map/psum | solution.py:65
  226.0 6.6 %collective-permute-done.7 = bf16[64,2048]{1,0:T(8,128)(2,1)S(1)} collective-permute-done((bf16[64,2048]{1,0:T(8,128)(2,1)S(1)}, bf16[64,2048]{1,0:T(8,128)(2,1)S(1)}, u32[]{:S(2)}, u32[]{:S(2)}) %collective-permute-start.7) | collective-permute-done | bytes 262176 | tf_op jit(solution)/shard_map/ppermute | solution.py:15
  235.2 6.4 %collective-permute-done.8 = bf16[64,2048]{1,0:T(8,128)(2,1)S(1)} collective-permute-done((bf16[64,2048]{1,0:T(8,128)(2,1)S(1)}, bf16[64,2048]{1,0:T(8,128)(2,1)S(1)}, u32[]{:S(2)}, u32[]{:S(2)}) %collective-permute-start.8) | collective-permute-done | bytes 262176 | tf_op jit(solution)/shard_map/ppermute | solution.py:15
  241.6 1.8 fusion.30
  243.5 5.8 %cholesky.55 = f32[64,64]{1,0:T(8,128)S(1)} custom-call(f32[64,64]{1,0:T(8,128)S(1)} %fusion.34), custom_call_target="Cholesky" | custom-call | tf_op jit(solution)/shard_map/jit(cholesky)/cholesky | solution.py:39
  250.6 4.9 %custom-call.7 = f32[1,64,64]{1,2,0:T(8,128)S(1)} custom-call(f32[1,64,64]{2,1,0:T(8,128)S(1)} %fusion.32), custom_call_target="InvertDiagBlocksLowerTriangular" | custom-call | tf_op jit(solution)/shard_map/triangular_solve/custom-call.0 | solution.py:40
  255.5 1.7 convolution_convert_fusion.2
  257.2 6.0 %fusion.40 = (bf16[64,2048]{1,0:T(8,128)(2,1)S(1)}, f32[64,2048]{1,0:T(8,128)S(1)}) fusion(bf16[64,2048]{1,0:T(8,128)(2,1)S(1)} %convolution_convert_fusion.2, bf16[2048,2048]{1,0:T(8,128)(2,1)} %subtract_convert_fusion.1), kind=kOutput, calls=%fused_computation.70 | convolution fusion | flops 537001984 | bytes 9437184 | tf_op jit(solution)/shard_map/dot_general | solution.py:69
  266.4 6.9 %collective-permute-done.10 = bf16[64,2048]{1,0:T(8,128)(2,1)S(1)} collective-permute-done((bf16[64,2048]{1,0:T(8,128)(2,1)S(1)}, bf16[64,2048]{1,0:T(8,128)(2,1)S(1)}, u32[]{:S(2)}, u32[]{:S(2)}) %collective-permute-start.10) | collective-permute-done | bytes 262176 | tf_op jit(solution)/shard_map/ppermute | solution.py:15
  273.4 1.5 collective-permute-start.11
  275.0 6.0 %collective-permute-done.11 = bf16[64,2048]{1,0:T(8,128)(2,1)S(1)} collective-permute-done((bf16[64,2048]{1,0:T(8,128)(2,1)S(1)}, bf16[64,2048]{1,0:T(8,128)(2,1)S(1)}, u32[]{:S(2)}, u32[]{:S(2)}) %collective-permute-start.11) | collective-permute-done | bytes 262176 | tf_op jit(solution)/shard_map/ppermute | solution.py:15
  281.0 6.9 %fusion.1 = bf16[1,2048,2048]{2,1,0:T(8,128)(2,1)} fusion(bf16[64,2048]{1,0:T(8,128)(2,1)S(1)} %convolution_convert_fusion.2, bf16[2048,2048]{1,0:T(8,128)(2,1)} %subtract_convert_fusion.1, f32[64,2048]{1,0:T(8,128)S(1)} %get-tuple-element.16, bf16[64,2048]{1,0:T(8,128)(2,1)S(1)} %collective-permute-done.11, ...), kind=kOutput, calls=%fused_computation.5 | convolution fusion | flops 554696704 | bytes 18350084 | tf_op jit(solution)/shard_map/dot_general | solution.py:73
  (50 shorter events, 20.7 us)
Async XLA Ops:
  6.5 33.1 %all-gather.5.cloned.1.call-start = ((), (), s32[]{:S(2)}) async-start(), calls=%async_computation.2 | async-start | bytes 1310720 | tf_op jit(solution)/shard_map/all_gather | solution.py:53
  8.4 46.8 %copy-start.2 = (bf16[2,64,2048]{2,1,0:T(8,128)(2,1)S(1)}, bf16[2,64,2048]{2,1,0:T(8,128)(2,1)}, u32[]{:S(2)}) copy-start(bf16[2,64,2048]{2,1,0:T(8,128)(2,1)} %param.11) | copy-start | bytes 1572868
  8.4 84.1 %all-reduce.3.cloned.1.call-start = ((), (), s32[]{:S(2)}) async-start(), calls=%async_computation | async-start | bytes 524288 | tf_op jit(solution)/shard_map/psum | solution.py:65
  51.8 3.4 %copy-start = (bf16[2048,2048]{1,0:T(8,128)(2,1)}, bf16[2048,2048]{1,0:T(8,128)(2,1)S(1)}, u32[]{:S(2)}) copy-start(bf16[2048,2048]{1,0:T(8,128)(2,1)S(1)} %get-tuple-element.11) | copy-start | bytes 25165828
  51.8 40.6 %copy-start.4 = (s32[2]{0:T(128)S(1)}, s32[2]{0:T(128)}, u32[]{:S(2)}) copy-start(s32[2]{0:T(128)} %param.12) | copy-start | bytes 28
  57.5 108.6 %all-gather.7.cloned.1.call-start = ((), (), s32[]{:S(2)}) async-start(), calls=%async_computation.3 | async-start | bytes 1310720 | tf_op jit(solution)/shard_map/all_gather | solution.py:53
  92.5 2.7 collective-permute-start
  96.2 8.8 %collective-permute-start.1 = (bf16[64,2048]{1,0:T(8,128)(2,1)S(1)}, bf16[64,2048]{1,0:T(8,128)(2,1)S(1)}, u32[]{:S(2)}, u32[]{:S(2)}) collective-permute-start(bf16[64,2048]{1,0:T(8,128)(2,1)S(1)} %fusion.11), channel_id=1, source_target_pairs={{0,8},{4,12},{8,0},{12,4},{16,24},{20,28},{24,16},{28,20},{1,9},{5... | collective-permute-start | bytes 786440 | tf_op jit(solution)/shard_map/ppermute | solution.py:15
  106.1 7.9 %collective-permute-start.2 = (bf16[64,2048]{1,0:T(8,128)(2,1)S(1)}, bf16[64,2048]{1,0:T(8,128)(2,1)S(1)}, u32[]{:S(2)}, u32[]{:S(2)}) collective-permute-start(bf16[64,2048]{1,0:T(8,128)(2,1)S(1)} %fusion.13), channel_id=1, source_target_pairs={{0,16},{4,20},{8,24},{12,28},{16,0},{20,4},{24,8},{28,12},{1,17},{... | collective-permute-start | bytes 786440 | tf_op jit(solution)/shard_map/ppermute | solution.py:15
  135.9 1.6 collective-permute-start.3
  137.5 8.4 %collective-permute-start.4 = (bf16[64,2048]{1,0:T(8,128)(2,1)S(1)}, bf16[64,2048]{1,0:T(8,128)(2,1)S(1)}, u32[]{:S(2)}, u32[]{:S(2)}) collective-permute-start(bf16[64,2048]{1,0:T(8,128)(2,1)S(1)} %fusion.15), channel_id=1, source_target_pairs={{0,8},{4,12},{8,0},{12,4},{16,24},{20,28},{24,16},{28,20},{1,9},{5... | collective-permute-start | bytes 786440 | tf_op jit(solution)/shard_map/ppermute | solution.py:15
  139.1 81.9 %all-reduce.5.cloned.1.call-start = ((), (), s32[]{:S(2)}) async-start(), calls=%async_computation.1 | async-start | bytes 524288 | tf_op jit(solution)/shard_map/psum | solution.py:65
  146.0 20.2 %copy-start.1 = (bf16[1,512,2048]{2,1,0:T(8,128)(2,1)S(1)}, bf16[1,512,2048]{2,1,0:T(8,128)(2,1)}, u32[]{:S(2)}) copy-start(bf16[1,512,2048]{2,1,0:T(8,128)(2,1)} %param.9) | copy-start | bytes 6291460
  146.0 7.6 %collective-permute-start.5 = (bf16[64,2048]{1,0:T(8,128)(2,1)S(1)}, bf16[64,2048]{1,0:T(8,128)(2,1)S(1)}, u32[]{:S(2)}, u32[]{:S(2)}) collective-permute-start(bf16[64,2048]{1,0:T(8,128)(2,1)S(1)} %fusion.16), channel_id=1, source_target_pairs={{0,16},{4,20},{8,24},{12,28},{16,0},{20,4},{24,8},{28,12},{1,17},{... | collective-permute-start | bytes 786440 | tf_op jit(solution)/shard_map/ppermute | solution.py:15
  166.2 14.0 %copy-start.3 = (bf16[2,64,2048]{2,1,0:T(8,128)(2,1)S(1)}, bf16[2,64,2048]{2,1,0:T(8,128)(2,1)}, u32[]{:S(2)}) copy-start(bf16[2,64,2048]{2,1,0:T(8,128)(2,1)} %param.11) | copy-start | bytes 1572868
  221.0 1.9 collective-permute-start.6
  223.8 8.8 %collective-permute-start.7 = (bf16[64,2048]{1,0:T(8,128)(2,1)S(1)}, bf16[64,2048]{1,0:T(8,128)(2,1)S(1)}, u32[]{:S(2)}, u32[]{:S(2)}) collective-permute-start(bf16[64,2048]{1,0:T(8,128)(2,1)S(1)} %fusion.12), channel_id=1, source_target_pairs={{0,8},{4,12},{8,0},{12,4},{16,24},{20,28},{24,16},{28,20},{1,9},{5... | collective-permute-start | bytes 786440 | tf_op jit(solution)/shard_map/ppermute | solution.py:15
  233.7 7.9 %collective-permute-start.8 = (bf16[64,2048]{1,0:T(8,128)(2,1)S(1)}, bf16[64,2048]{1,0:T(8,128)(2,1)S(1)}, u32[]{:S(2)}, u32[]{:S(2)}) collective-permute-start(bf16[64,2048]{1,0:T(8,128)(2,1)S(1)} %fusion.14), channel_id=1, source_target_pairs={{0,16},{4,20},{8,24},{12,28},{16,0},{20,4},{24,8},{28,12},{1,17},{... | collective-permute-start | bytes 786440 | tf_op jit(solution)/shard_map/ppermute | solution.py:15
  263.3 1.6 collective-permute-start.9
  264.9 8.4 %collective-permute-start.10 = (bf16[64,2048]{1,0:T(8,128)(2,1)S(1)}, bf16[64,2048]{1,0:T(8,128)(2,1)S(1)}, u32[]{:S(2)}, u32[]{:S(2)}) collective-permute-start(bf16[64,2048]{1,0:T(8,128)(2,1)S(1)} %fusion.17), channel_id=1, source_target_pairs={{0,8},{4,12},{8,0},{12,4},{16,24},{20,28},{24,16},{28,20},{1,9},{5... | collective-permute-start | bytes 786440 | tf_op jit(solution)/shard_map/ppermute | solution.py:15
  273.4 7.6 %collective-permute-start.11 = (bf16[64,2048]{1,0:T(8,128)(2,1)S(1)}, bf16[64,2048]{1,0:T(8,128)(2,1)S(1)}, u32[]{:S(2)}, u32[]{:S(2)}) collective-permute-start(bf16[64,2048]{1,0:T(8,128)(2,1)S(1)} %fusion.18), channel_id=1, source_target_pairs={{0,16},{4,20},{8,24},{12,28},{16,0},{20,4},{24,8},{28,12},{1,17},{... | collective-permute-start | bytes 786440 | tf_op jit(solution)/shard_map/ppermute | solution.py:15
Sparse Core Ops, SparseCore 0:
  8.9 30.6 all-gather.4
  57.7 34.7 all-reduce.2
  139.2 26.9 all-gather.6
  186.0 34.9 all-reduce.4
where the time goes:
time: 295 us; the launch traced here: 294 us
  waiting for transfers between devices  161 us (55%)
  matrix products  67 us (23%)
  other arithmetic  28.6 us (10%)
  between operations  18.6 us (6%)
  starting transfers between devices  12.7 us (4%)
  local copies, waits for them, and re-layouts  6.03 us (2%)
    psum x2, waiting for transfers between devices, per_device(): lax.psum(local_left.astype(jnp.bfloat16), 'tensor').astype(jnp.float32)  70 us
    ppermute x12, waiting for transfers between devices, from_partner(): return lax.ppermute(value, axis, pairs)  54.5 us
    all_gather x2, waiting for transfers between devices, per_device(): lax.all_gather(grads_step, 'tensor', axis=1, tiled=True)  36.8 us
    dot_general x2, matrix products, per_device(): lax.dot_general(hidden_step, lax.all_gather(grads_step, 'tensor', axis=1,...  26.2 us
    dot_general x2, matrix products, per_device(): lax.dot_general(right_diff, ortho_bf, (((0,), (0,)), ((), ())), preferred...  13.8 us
    another operation x6, other arithmetic, orthonormal(): lower_factor = jnp.linalg.cholesky(gram_matrix)  13.1 us
    ppermute x12, starting transfers between devices, from_partner(): return lax.ppermute(value, axis, pairs)  12.4 us
    dot_general x2, matrix products, per_device(): lax.dot_general(ortho_bf, updated, (((1,), (1,)), ((), ())), preferred_el...  12.1 us
  transfers between devices with their start and end apart: 16, of which 14 were waited for; matrix products, arithmetic and copies ran while one was open for 3% of the time, Pallas kernels for 0%

commit v1 on v0

--- a/solution.py
+++ b/solution.py
@@ -62,7 +62,9 @@
         start_factor = factor_start[step_index]
         pairing = matching[step_index]
         local_left = jnp.dot(start_factor, updated, preferred_element_type=jnp.float32)
-        left_total = lax.psum(local_left.astype(jnp.bfloat16), "tensor").astype(jnp.float32)
+        left_total = jnp.sum(
+            lax.all_gather(local_left.astype(jnp.bfloat16), "tensor"), axis=0
+        ).astype(jnp.float32)
         left_diff = left_total - swap_left_side(left_total, pairing)
         gram_matrix = jnp.dot(left_diff, left_diff.T, precision=lax.Precision.HIGHEST)
         ortho_bf = orthonormal(gram_matrix, left_diff).astype(jnp.bfloat16)

time: 295 us -> 274 us (0.929)
  waiting for transfers between devices: 161 us -> 146 us
  matrix products: 67 us -> 63 us
    psum x2 -> x0, waiting for transfers between devices: 70 us -> none  [per_device(): lax.psum(local_left.astype(jnp.bfloat16), 'tensor').astype(jnp.float32)]
    all_gather x0 -> x2, waiting for transfers between devices: none -> 55 us  [per_device(): lax.all_gather(local_left.astype(jnp.bfloat16), 'tensor')]
    convert_element_type x4, other arithmetic: 4.13 us -> 0.33 us  [swap_left_side(): payload.astype(jnp.bfloat16)]
where the time goes in v1:
time: 274 us
  waiting for transfers between devices  146 us (53%)
  matrix products  63 us (23%)
  other arithmetic  27.6 us (10%)
  between operations  18.4 us (7%)
  starting transfers between devices  12.9 us (5%)
  local copies, waits for them, and re-layouts  6.03 us (2%)
    all_gather x2, waiting for transfers between devices, per_device(): lax.all_gather(local_left.astype(jnp.bfloat16), 'tensor')  55 us
    ppermute x12, waiting for transfers between devices, from_partner(): return lax.ppermute(value, axis, pairs)  54.5 us
    all_gather x2, waiting for transfers between devices, per_device(): lax.all_gather(grads_step, 'tensor', axis=1, tiled=True)  36.4 us
    dot_general x2, matrix products, per_device(): lax.dot_general(hidden_step, lax.all_gather(grads_step, 'tensor', axis=1,...  26.2 us
    dot_general x2, matrix products, per_device(): lax.dot_general(right_diff, ortho_bf, (((0,), (0,)), ((), ())), preferred...  13.8 us
    another operation x6, other arithmetic, orthonormal(): lower_factor = jnp.linalg.cholesky(gram_matrix)  13.1 us
    ppermute x12, starting transfers between devices, from_partner(): return lax.ppermute(value, axis, pairs)  12.6 us
    dot_general x2, matrix products, per_device(): lax.dot_general(ortho_bf, updated, (((1,), (1,)), ((), ())), preferred_el...  12.1 us
  transfers between devices with their start and end apart: 16, of which 14 were waited for; matrix products, arithmetic and copies ran while one was open for 3% of the time, Pallas kernels for 0%

profile of v1, /device:TPU:0, one launch (start us, length us, event | category | flops | bytes accessed | tf_op | source)
XLA Modules:
  0.0 273.8 jit_solution(3955755211666089733)
XLA Ops:
  6.5 1.9 fusion.37
  8.5 31.2 %all-gather.9.cloned.1.call-done = bf16[1,256,2048]{2,1,0:T(8,128)(2,1)} async-done(((bf16[1,256,512]{2,1,0:T(8,128)(2,1)}), bf16[1,256,2048]{2,1,0:T(8,128)(2,1)}) %all-gather.9.cloned.1.call-update) | async-done | bytes 1048592 | tf_op jit(solution)/shard_map/all_gather | solution.py:53
  39.6 12.2 %fusion = (bf16[2048,2048]{1,0:T(8,128)(2,1)S(1)}, f32[2048,2048]{1,0:T(8,128)}) fusion(bf16[1,2048,2048]{2,1,0:T(8,128)(2,1)} %param.8, bf16[1,256,2048]{2,1,0:T(8,128)(2,1)} %all-gather.9.cloned.1.call-done, bf16[1,512,2048]{2,1,0:T(8,128)(2,1)} %param.9), kind=kOutput, calls=%fused_computation.1 | convolution fusion | flops 2164260864 | bytes 35651584 | tf_op jit(solution)/shard_map/dot_general | solution.py:51
  51.8 3.4 %copy-done = bf16[2048,2048]{1,0:T(8,128)(2,1)} copy-done((bf16[2048,2048]{1,0:T(8,128)(2,1)}, bf16[2048,2048]{1,0:T(8,128)(2,1)S(1)}, u32[]{:S(2)}) %copy-start) | copy-done | bytes 8388632
  55.2 2.3 fusion.2
  57.6 27.5 %all-gather.11.cloned.1.call-done = bf16[256,2048]{1,0:T(8,128)(2,1)} async-done(((bf16[64,2048]{1,0:T(8,128)(2,1)}), bf16[256,2048]{1,0:T(8,128)(2,1)}) %all-gather.11.cloned.1.call-update) | async-done | bytes 1048592 | tf_op jit(solution)/shard_map/all_gather | solution.py:66
  91.4 6.6 %collective-permute-done.1 = bf16[64,2048]{1,0:T(8,128)(2,1)S(1)} collective-permute-done((bf16[64,2048]{1,0:T(8,128)(2,1)S(1)}, bf16[64,2048]{1,0:T(8,128)(2,1)S(1)}, u32[]{:S(2)}, u32[]{:S(2)}) %collective-permute-start.1) | collective-permute-done | bytes 262176 | tf_op jit(solution)/shard_map/ppermute | solution.py:15
  98.0 1.5 collective-permute-start.2
  99.6 6.4 %collective-permute-done.2 = bf16[64,2048]{1,0:T(8,128)(2,1)S(1)} collective-permute-done((bf16[64,2048]{1,0:T(8,128)(2,1)S(1)}, bf16[64,2048]{1,0:T(8,128)(2,1)S(1)}, u32[]{:S(2)}, u32[]{:S(2)}) %collective-permute-start.2) | collective-permute-done | bytes 262176 | tf_op jit(solution)/shard_map/ppermute | solution.py:15
  106.8 5.8 %cholesky.44 = f32[64,64]{1,0:T(8,128)S(1)} custom-call(f32[64,64]{1,0:T(8,128)S(1)} %fusion.36), custom_call_target="Cholesky" | custom-call | tf_op jit(solution)/shard_map/jit(cholesky)/cholesky | solution.py:39
  114.0 4.9 %custom-call.6 = f32[1,64,64]{1,2,0:T(8,128)S(1)} custom-call(f32[1,64,64]{2,1,0:T(8,128)S(1)} %fusion.31), custom_call_target="InvertDiagBlocksLowerTriangular" | custom-call | tf_op jit(solution)/shard_map/triangular_solve/custom-call.0 | solution.py:40
  119.7 6.0 %fusion.39 = (bf16[64,2048]{1,0:T(8,128)(2,1)S(1)}, f32[64,2048]{1,0:T(8,128)S(1)}) fusion(bf16[64,2048]{1,0:T(8,128)(2,1)S(1)} %convolution_convert_fusion.3, bf16[2048,2048]{1,0:T(8,128)(2,1)} %copy-done), kind=kOutput, calls=%fused_computation.69 | convolution fusion | flops 537001984 | bytes 9437184 | tf_op jit(solution)/shard_map/dot_general | solution.py:71
  127.3 1.5 collective-permute-start.4
  129.1 6.6 %collective-permute-done.4 = bf16[64,2048]{1,0:T(8,128)(2,1)S(1)} collective-permute-done((bf16[64,2048]{1,0:T(8,128)(2,1)S(1)}, bf16[64,2048]{1,0:T(8,128)(2,1)S(1)}, u32[]{:S(2)}, u32[]{:S(2)}) %collective-permute-start.4) | collective-permute-done | bytes 262176 | tf_op jit(solution)/shard_map/ppermute | solution.py:15
  135.9 1.5 collective-permute-start.5
  137.4 6.0 %collective-permute-done.5 = bf16[64,2048]{1,0:T(8,128)(2,1)S(1)} collective-permute-done((bf16[64,2048]{1,0:T(8,128)(2,1)S(1)}, bf16[64,2048]{1,0:T(8,128)(2,1)S(1)}, u32[]{:S(2)}, u32[]{:S(2)}) %collective-permute-start.5) | collective-permute-done | bytes 262176 | tf_op jit(solution)/shard_map/ppermute | solution.py:15
  143.4 6.9 %subtract_convert_fusion.2 = bf16[2048,2048]{1,0:T(8,128)(2,1)} fusion(bf16[2048,2048]{1,0:T(8,128)(2,1)} %copy-done, bf16[64,2048]{1,0:T(8,128)(2,1)S(1)} %convolution_convert_fusion.3, f32[64,2048]{1,0:T(8,128)S(1)} %get-tuple-element.14, bf16[64,2048]{1,0:T(8,128)(2,1)S(1)} %collective-permute-done.5, bf16[64,2048]{1,0:T(8,128)(2,1)S(1)} %collective-permute-done.3, ...), kind=kOutput, calls=%fused_computation.4 | convolution fusion | flops 554696704 | bytes 18350084 | tf_op jit(solution)/shard_map/dot_general | solution.py:75
  150.3 5.2 %all-gather.13.cloned.1.call-done = bf16[1,256,2048]{2,1,0:T(8,128)(2,1)} async-done(((bf16[1,256,512]{2,1,0:T(8,128)(2,1)}), bf16[1,256,2048]{2,1,0:T(8,128)(2,1)}) %all-gather.13.cloned.1.call-update) | async-done | bytes 1048592 | tf_op jit(solution)/shard_map/all_gather | solution.py:53
  155.5 14.0 %subtract_convert_fusion.1 = bf16[2048,2048]{1,0:T(8,128)(2,1)} fusion(f32[2048,2048]{1,0:T(8,128)} %get-tuple-element.12, bf16[2048,2048]{1,0:T(8,128)(2,1)} %subtract_convert_fusion.2, bf16[1,256,2048]{2,1,0:T(8,128)(2,1)} %all-gather.13.cloned.1.call-done, bf16[1,512,2048]{2,1,0:T(8,128)(2,1)S(1)} %copy-done.1), kind=kOutput, calls=%fused_computation.3 | convolution fusion | flops 2172649472 | bytes 35651584 | tf_op jit(solution)/shard_map/dot_general | solution.py:51
  169.5 5.7 %fusion.3 = bf16[64,2048]{1,0:T(8,128)(2,1)} fusion(bf16[2048,2048]{1,0:T(8,128)(2,1)} %subtract_convert_fusion.1, bf16[2,64,2048]{2,1,0:T(8,128)(2,1)S(1)} %copy-done.3), kind=kOutput, calls=%fused_computation.11 | convolution fusion | flops 537001984 | bytes 8912896 | tf_op jit(solution)/shard_map/dot_general | solution.py:64
  175.2 27.5 %all-gather.15.cloned.1.call-done = bf16[256,2048]{1,0:T(8,128)(2,1)} async-done(((bf16[64,2048]{1,0:T(8,128)(2,1)}), bf16[256,2048]{1,0:T(8,128)(2,1)}) %all-gather.15.cloned.1.call-update) | async-done | bytes 1048592 | tf_op jit(solution)/shard_map/all_gather | solution.py:66
  206.1 1.5 collective-permute-start.7
  208.3 6.6 %collective-permute-done.7 = bf16[64,2048]{1,0:T(8,128)(2,1)S(1)} collective-permute-done((bf16[64,2048]{1,0:T(8,128)(2,1)S(1)}, bf16[64,2048]{1,0:T(8,128)(2,1)S(1)}, u32[]{:S(2)}, u32[]{:S(2)}) %collective-permute-start.7) | collective-permute-done | bytes 262176 | tf_op jit(solution)/shard_map/ppermute | solution.py:15
  215.0 1.5 collective-permute-start.8
  216.5 6.4 %collective-permute-done.8 = bf16[64,2048]{1,0:T(8,128)(2,1)S(1)} collective-permute-done((bf16[64,2048]{1,0:T(8,128)(2,1)S(1)}, bf16[64,2048]{1,0:T(8,128)(2,1)S(1)}, u32[]{:S(2)}, u32[]{:S(2)}) %collective-permute-start.8) | collective-permute-done | bytes 262176 | tf_op jit(solution)/shard_map/ppermute | solution.py:15
  223.8 5.8 %cholesky.55 = f32[64,64]{1,0:T(8,128)S(1)} custom-call(f32[64,64]{1,0:T(8,128)S(1)} %fusion.34), custom_call_target="Cholesky" | custom-call | tf_op jit(solution)/shard_map/jit(cholesky)/cholesky | solution.py:39
  231.0 4.9 %custom-call.7 = f32[1,64,64]{1,2,0:T(8,128)S(1)} custom-call(f32[1,64,64]{2,1,0:T(8,128)S(1)} %fusion.32), custom_call_target="InvertDiagBlocksLowerTriangular" | custom-call | tf_op jit(solution)/shard_map/triangular_solve/custom-call.0 | solution.py:40
  236.6 6.0 %fusion.40 = (bf16[64,2048]{1,0:T(8,128)(2,1)S(1)}, f32[64,2048]{1,0:T(8,128)S(1)}) fusion(bf16[64,2048]{1,0:T(8,128)(2,1)S(1)} %convolution_convert_fusion.2, bf16[2048,2048]{1,0:T(8,128)(2,1)} %subtract_convert_fusion.1), kind=kOutput, calls=%fused_computation.70 | convolution fusion | flops 537001984 | bytes 9437184 | tf_op jit(solution)/shard_map/dot_general | solution.py:71
  245.8 6.9 %collective-permute-done.10 = bf16[64,2048]{1,0:T(8,128)(2,1)S(1)} collective-permute-done((bf16[64,2048]{1,0:T(8,128)(2,1)S(1)}, bf16[64,2048]{1,0:T(8,128)(2,1)S(1)}, u32[]{:S(2)}, u32[]{:S(2)}) %collective-permute-start.10) | collective-permute-done | bytes 262176 | tf_op jit(solution)/shard_map/ppermute | solution.py:15
  252.8 1.5 collective-permute-start.11
  254.3 6.0 %collective-permute-done.11 = bf16[64,2048]{1,0:T(8,128)(2,1)S(1)} collective-permute-done((bf16[64,2048]{1,0:T(8,128)(2,1)S(1)}, bf16[64,2048]{1,0:T(8,128)(2,1)S(1)}, u32[]{:S(2)}, u32[]{:S(2)}) %collective-permute-start.11) | collective-permute-done | bytes 262176 | tf_op jit(solution)/shard_map/ppermute | solution.py:15
  260.3 6.9 %fusion.1 = bf16[1,2048,2048]{2,1,0:T(8,128)(2,1)} fusion(bf16[64,2048]{1,0:T(8,128)(2,1)S(1)} %convolution_convert_fusion.2, bf16[2048,2048]{1,0:T(8,128)(2,1)} %subtract_convert_fusion.1, f32[64,2048]{1,0:T(8,128)S(1)} %get-tuple-element.16, bf16[64,2048]{1,0:T(8,128)(2,1)S(1)} %collective-permute-done.11, ...), kind=kOutput, calls=%fused_computation.5 | convolution fusion | flops 554696704 | bytes 18350084 | tf_op jit(solution)/shard_map/dot_general | solution.py:75
  (52 shorter events, 16.6 us)
Async XLA Ops:
  6.5 33.1 %all-gather.9.cloned.1.call-start = ((), (), s32[]{:S(2)}) async-start(), calls=%async_computation | async-start | bytes 1310720 | tf_op jit(solution)/shard_map/all_gather | solution.py:53
  8.4 46.8 %copy-start.2 = (bf16[2,64,2048]{2,1,0:T(8,128)(2,1)S(1)}, bf16[2,64,2048]{2,1,0:T(8,128)(2,1)}, u32[]{:S(2)}) copy-start(bf16[2,64,2048]{2,1,0:T(8,128)(2,1)} %param.11) | copy-start | bytes 1572868
  8.4 76.7 %all-gather.11.cloned.1.call-start = ((), (), s32[]{:S(2)}) async-start(), calls=%async_computation.1 | async-start | bytes 1310720 | tf_op jit(solution)/shard_map/all_gather | solution.py:66
  51.8 3.4 %copy-start = (bf16[2048,2048]{1,0:T(8,128)(2,1)}, bf16[2048,2048]{1,0:T(8,128)(2,1)S(1)}, u32[]{:S(2)}) copy-start(bf16[2048,2048]{1,0:T(8,128)(2,1)S(1)} %get-tuple-element.11) | copy-start | bytes 25165828
  55.2 31.3 %copy-start.4 = (s32[2]{0:T(128)S(1)}, s32[2]{0:T(128)}, u32[]{:S(2)}) copy-start(s32[2]{0:T(128)} %param.12) | copy-start | bytes 28
  57.6 97.9 %all-gather.13.cloned.1.call-start = ((), (), s32[]{:S(2)}) async-start(), calls=%async_computation.2 | async-start | bytes 1310720 | tf_op jit(solution)/shard_map/all_gather | solution.py:53
  86.5 2.6 collective-permute-start
  89.2 8.8 %collective-permute-start.1 = (bf16[64,2048]{1,0:T(8,128)(2,1)S(1)}, bf16[64,2048]{1,0:T(8,128)(2,1)S(1)}, u32[]{:S(2)}, u32[]{:S(2)}) collective-permute-start(bf16[64,2048]{1,0:T(8,128)(2,1)S(1)} %fusion.11), channel_id=1, source_target_pairs={{0,8},{4,12},{8,0},{12,4},{16,24},{20,28},{24,16},{28,20},{1,9},{5... | collective-permute-start | bytes 786440 | tf_op jit(solution)/shard_map/ppermute | solution.py:15
  98.0 7.9 %collective-permute-start.2 = (bf16[64,2048]{1,0:T(8,128)(2,1)S(1)}, bf16[64,2048]{1,0:T(8,128)(2,1)S(1)}, u32[]{:S(2)}, u32[]{:S(2)}) collective-permute-start(bf16[64,2048]{1,0:T(8,128)(2,1)S(1)} %fusion.13), channel_id=1, source_target_pairs={{0,16},{4,20},{8,24},{12,28},{16,0},{20,4},{24,8},{28,12},{1,17},{... | collective-permute-start | bytes 786440 | tf_op jit(solution)/shard_map/ppermute | solution.py:15
  125.7 1.6 collective-permute-start.3
  127.3 8.4 %collective-permute-start.4 = (bf16[64,2048]{1,0:T(8,128)(2,1)S(1)}, bf16[64,2048]{1,0:T(8,128)(2,1)S(1)}, u32[]{:S(2)}, u32[]{:S(2)}) collective-permute-start(bf16[64,2048]{1,0:T(8,128)(2,1)S(1)} %fusion.15), channel_id=1, source_target_pairs={{0,8},{4,12},{8,0},{12,4},{16,24},{20,28},{24,16},{28,20},{1,9},{5... | collective-permute-start | bytes 786440 | tf_op jit(solution)/shard_map/ppermute | solution.py:15
  128.9 73.8 %all-gather.15.cloned.1.call-start = ((), (), s32[]{:S(2)}) async-start(), calls=%async_computation.3 | async-start | bytes 1310720 | tf_op jit(solution)/shard_map/all_gather | solution.py:66
  135.8 19.7 %copy-start.1 = (bf16[1,512,2048]{2,1,0:T(8,128)(2,1)S(1)}, bf16[1,512,2048]{2,1,0:T(8,128)(2,1)}, u32[]{:S(2)}) copy-start(bf16[1,512,2048]{2,1,0:T(8,128)(2,1)} %param.9) | copy-start | bytes 6291460
  135.9 7.6 %collective-permute-start.5 = (bf16[64,2048]{1,0:T(8,128)(2,1)S(1)}, bf16[64,2048]{1,0:T(8,128)(2,1)S(1)}, u32[]{:S(2)}, u32[]{:S(2)}) collective-permute-start(bf16[64,2048]{1,0:T(8,128)(2,1)S(1)} %fusion.16), channel_id=1, source_target_pairs={{0,16},{4,20},{8,24},{12,28},{16,0},{20,4},{24,8},{28,12},{1,17},{... | collective-permute-start | bytes 786440 | tf_op jit(solution)/shard_map/ppermute | solution.py:15
  155.5 14.0 %copy-start.3 = (bf16[2,64,2048]{2,1,0:T(8,128)(2,1)S(1)}, bf16[2,64,2048]{2,1,0:T(8,128)(2,1)}, u32[]{:S(2)}) copy-start(bf16[2,64,2048]{2,1,0:T(8,128)(2,1)} %param.11) | copy-start | bytes 1572868
  204.1 1.9 collective-permute-start.6
  206.1 8.8 %collective-permute-start.7 = (bf16[64,2048]{1,0:T(8,128)(2,1)S(1)}, bf16[64,2048]{1,0:T(8,128)(2,1)S(1)}, u32[]{:S(2)}, u32[]{:S(2)}) collective-permute-start(bf16[64,2048]{1,0:T(8,128)(2,1)S(1)} %fusion.12), channel_id=1, source_target_pairs={{0,8},{4,12},{8,0},{12,4},{16,24},{20,28},{24,16},{28,20},{1,9},{5... | collective-permute-start | bytes 786440 | tf_op jit(solution)/shard_map/ppermute | solution.py:15
  215.0 7.9 %collective-permute-start.8 = (bf16[64,2048]{1,0:T(8,128)(2,1)S(1)}, bf16[64,2048]{1,0:T(8,128)(2,1)S(1)}, u32[]{:S(2)}, u32[]{:S(2)}) collective-permute-start(bf16[64,2048]{1,0:T(8,128)(2,1)S(1)} %fusion.14), channel_id=1, source_target_pairs={{0,16},{4,20},{8,24},{12,28},{16,0},{20,4},{24,8},{28,12},{1,17},{... | collective-permute-start | bytes 786440 | tf_op jit(solution)/shard_map/ppermute | solution.py:15
  242.6 1.6 collective-permute-start.9
  244.3 8.4 %collective-permute-start.10 = (bf16[64,2048]{1,0:T(8,128)(2,1)S(1)}, bf16[64,2048]{1,0:T(8,128)(2,1)S(1)}, u32[]{:S(2)}, u32[]{:S(2)}) collective-permute-start(bf16[64,2048]{1,0:T(8,128)(2,1)S(1)} %fusion.17), channel_id=1, source_target_pairs={{0,8},{4,12},{8,0},{12,4},{16,24},{20,28},{24,16},{28,20},{1,9},{5... | collective-permute-start | bytes 786440 | tf_op jit(solution)/shard_map/ppermute | solution.py:15
  252.8 7.6 %collective-permute-start.11 = (bf16[64,2048]{1,0:T(8,128)(2,1)S(1)}, bf16[64,2048]{1,0:T(8,128)(2,1)S(1)}, u32[]{:S(2)}, u32[]{:S(2)}) collective-permute-start(bf16[64,2048]{1,0:T(8,128)(2,1)S(1)} %fusion.18), channel_id=1, source_target_pairs={{0,16},{4,20},{8,24},{12,28},{16,0},{20,4},{24,8},{28,12},{1,17},{... | collective-permute-start | bytes 786440 | tf_op jit(solution)/shard_map/ppermute | solution.py:15
Sparse Core Ops, SparseCore 0:
  8.9 30.6 all-gather.8
  57.7 27.3 all-gather.10
  129.0 26.4 all-gather.12
  175.3 27.3 all-gather.14
